TPU v7x, 512 devices: a whole 4x4x16 slice. The times are simulated.
512 devices in a mesh: kv: 8 (over x, core), pool: 64 (over y, z).
Axes of the slice: x: 4, y: 4, z: 16, core: 2. Of those that a mesh axis runs over, the one named last changes fastest.
Arguments:
- hidden: bfloat16 [64, 2048], P('pool'), may hold values from -6 to 6
- norm_attn: bfloat16 [2048], replicated, may hold values from 0.099609375 to 1.8984375
- wq: bfloat16 [2048, 2048], P(None, 'kv'), may hold values from -0.125 to 0.125
- wkv: bfloat16 [2, 2048, 1024], P(None, None, 'kv'), may hold values from -0.125 to 0.125
- wo: bfloat16 [2048, 2048], P('kv'), may hold values from -0.125 to 0.125
- cache: bfloat16 [2, 1024, 128, 1024], P(None, 'pool', None, 'kv'), may hold values from -70 to 70, as said below
- slot_entry: int32 [1024], P('pool'), may hold values from -1 to 4095, as said below
- lengths: int32 [64], replicated, may hold values from 1 to 8192, as said below
- norm_mlp: bfloat16 [2048], replicated, may hold values from 0.099609375 to 1.8984375
- w_gate: bfloat16 [2048, 8192], P('pool', 'kv'), may hold values from -0.125 to 0.125
- w_up: bfloat16 [2048, 8192], P('pool', 'kv'), may hold values from -0.125 to 0.125
- w_down: bfloat16 [8192, 2048], P('kv', 'pool'), may hold values from -0.0625 to 0.0625
Outputs:
- output: bfloat16 [64, 2048], P('pool')
Inputs may be any that keep to these rules, and one draw needn't show every extreme that they name: slot_entry[s] is -1 for a free slot, else r * 64 + b: the slot holds block b of request r, that is its cached positions b * 128 to b * 128 + 127 that lie below lengths[r]. Every block of every request below ceil(lengths[r] / 128) sits in exactly one slot, anywhere in the pool; a holder's slots are its 16 entries. Its new token stands at position lengths[r]. `cache`: keys and values of the cached tokens, already rotated.
All inputs are finite; a program needn't handle non-finite values.
Results may differ from a plain program's by a relative error of at most 0.012.
The roundings to bfloat16 on the way count: a program that leaves them out, or rounds other values in their place, can miss the bound.
Values may be sent and summed in bfloat16 or wider, within the bound.
A program may use at most 64 MiB of HBM per device.

v0:
```python
import math

import jax
import jax.numpy as jnp
from jax import lax
from jax.sharding import PartitionSpec as P

QUERY_HEAD_COUNT = 16
KEY_VALUE_HEADS = 8
HEAD_SIZE = 128


NEGATIVE = -1e30
EPSILON = 1e-05
ROPE_BASE = 1000000.0


def combined_all(x, axis, combine):
    everything = jax.tree.map(lambda part: lax.all_gather(part, axis), x)
    initial = jax.tree.map(lambda part: part[0], everything)

    def step(k, so_far):
        return combine(so_far, jax.tree.map(lambda part: part[k], everything))

    return lax.fori_loop(1, lax.axis_size(axis), step, initial)


def narrow_rows(tensor):
    return lax.optimization_barrier(tensor.astype(jnp.bfloat16))


def rms_scale(inputs, gain_vec):
    widened = inputs.astype(jnp.float32)
    mean_square = jnp.mean(widened * widened, axis=-1, keepdims=True)
    return narrow_rows(widened * lax.rsqrt(mean_square + EPSILON) * gain_vec.astype(jnp.float32))


def rotate(vectors, positions):
    head_width = vectors.shape[-1]
    halfway = head_width // 2
    frequency = jnp.exp(
        jnp.arange(halfway, dtype=jnp.float32) * (-2.0 * math.log(ROPE_BASE) / head_width)
    )
    angles = positions.astype(jnp.float32)[:, None] * frequency[None, :]
    cosine = jnp.cos(angles)[:, None, :]
    sine_of = jnp.sin(angles)[:, None, :]
    leading = vectors[..., :halfway]
    trailing = vectors[..., halfway:]
    return jnp.concatenate(
        [leading * cosine - trailing * sine_of, trailing * cosine + leading * sine_of], axis=-1
    )


def combine(earlier, latter):
    highest = jnp.maximum(earlier[0], latter[0])
    scale_early = jnp.exp(earlier[0] - highest)
    scale_late = jnp.exp(latter[0] - highest)
    row_count, head_count = highest.shape
    feature = earlier[2].shape[1] // head_count
    early_out = earlier[2].reshape(row_count, head_count, feature) * scale_early[:, :, None]
    late_out = latter[2].reshape(row_count, head_count, feature) * scale_late[:, :, None]
    weight_sum = earlier[1] * scale_early + latter[1] * scale_late
    return (highest, weight_sum, (early_out + late_out).reshape(row_count, head_count * feature))


def per_device(
    hidden, norm_attn, wq, wkv, wo, cache, slot_entry, lengths, norm_mlp, w_gate, w_up, w_down
):
    home_rows = hidden.shape[0]
    shared_heads = wkv.shape[2] // HEAD_SIZE
    queries_per_shared = QUERY_HEAD_COUNT // KEY_VALUE_HEADS
    query_heads = shared_heads * queries_per_shared
    home_index = lax.axis_index("pool")
    max_blocks = slot_entry.shape[0] * lax.axis_size("pool") // 16
    positions = lax.dynamic_slice_in_dim(lengths, home_index * home_rows, home_rows)
    normed_input = rms_scale(hidden, norm_attn)
    query_rows = jnp.dot(normed_input, wq, preferred_element_type=jnp.float32).reshape(
        home_rows, query_heads, HEAD_SIZE
    )
    query_rows = narrow_rows(rotate(query_rows, positions) * HEAD_SIZE ** (-0.5))
    fresh_keys = jnp.dot(normed_input, wkv[0], preferred_element_type=jnp.float32).reshape(
        home_rows, shared_heads, HEAD_SIZE
    )
    fresh_keys = narrow_rows(rotate(fresh_keys, positions))
    fresh_values = narrow_rows(
        jnp.dot(normed_input, wkv[1], preferred_element_type=jnp.float32)
    ).reshape(home_rows, shared_heads, HEAD_SIZE)
    every_query = lax.all_gather(
        query_rows.reshape(home_rows, query_heads * HEAD_SIZE), "pool", axis=0, tiled=True
    )
    request_list = every_query.shape[0]
    every_query = every_query.reshape(request_list, shared_heads, queries_per_shared, HEAD_SIZE)
    slot_count = slot_entry.shape[0]
    block_len = cache.shape[2]
    live_slot = slot_entry >= 0
    owners = jnp.where(live_slot, slot_entry // max_blocks, 0)
    block_index = jnp.where(live_slot, slot_entry % max_blocks, 0)
    picked = every_query[owners]
    block_keys = cache[0].reshape(slot_count, block_len, shared_heads, HEAD_SIZE)
    block_values = cache[1].reshape(slot_count, block_len, shared_heads, HEAD_SIZE)
    scores = jnp.einsum("sgjd,stgd->sgjt", picked, block_keys, preferred_element_type=jnp.float32)
    position = block_index[:, None] * block_len + jnp.arange(block_len, dtype=jnp.int32)[None, :]
    in_range = live_slot[:, None] & (position < lengths[owners][:, None])
    scores = jnp.where(in_range[:, None, None, :], scores, NEGATIVE)
    block_max = jnp.max(scores, axis=-1)
    same_owner = (owners[:, None] == owners[None, :]) & live_slot[:, None] & live_slot[None, :]
    holder_max = jnp.max(jnp.where(same_owner[:, :, None, None], block_max[None], NEGATIVE), axis=1)
    raised = jnp.where(in_range[:, None, None, :], jnp.exp(scores - holder_max[..., None]), 0.0)
    holder_total = jnp.sum(raised, axis=-1)
    holder_output = jnp.einsum(
        "sgjt,stgd->sgjd", narrow_rows(raised), block_values, preferred_element_type=jnp.float32
    )
    member = (owners[:, None] == jnp.arange(request_list, dtype=jnp.int32)[None, :]) & live_slot[
        :, None
    ]
    request_max = jnp.max(jnp.where(member.T[:, :, None, None], holder_max[None], NEGATIVE), axis=1)
    request_max = request_max.reshape(request_list, query_heads)
    member_float = member.astype(jnp.float32)
    request_total = jnp.einsum(
        "sr,sgj->rgj", member_float, holder_total, precision=lax.Precision.HIGHEST
    )
    request_total = request_total.reshape(request_list, query_heads)
    request_out = jnp.einsum(
        "sr,sgjd->rgjd", member_float, holder_output, precision=lax.Precision.HIGHEST
    )
    request_out = request_out.reshape(request_list, query_heads * HEAD_SIZE)
    merged = combined_all((request_max, request_total, request_out), "pool", combine)
    part_max = lax.dynamic_slice_in_dim(merged[0], home_index * home_rows, home_rows)
    part_total = lax.dynamic_slice_in_dim(merged[1], home_index * home_rows, home_rows)
    part_out = lax.dynamic_slice_in_dim(merged[2], home_index * home_rows, home_rows)
    own_query = query_rows.reshape(home_rows, shared_heads, queries_per_shared, HEAD_SIZE).astype(
        jnp.float32
    )
    new_score = jnp.sum(own_query * fresh_keys.astype(jnp.float32)[:, :, None, :], axis=-1).reshape(
        home_rows, query_heads
    )
    highest = jnp.maximum(part_max, new_score)
    old_scale = jnp.exp(part_max - highest)
    new_scale = jnp.exp(new_score - highest)
    weight_sum = part_total * old_scale + new_scale
    new_term = (
        new_scale.reshape(home_rows, shared_heads, queries_per_shared)[..., None]
        * fresh_values.astype(jnp.float32)[:, :, None, :]
    )
    combined = part_out.reshape(home_rows, query_heads, HEAD_SIZE) * old_scale[
        ..., None
    ] + new_term.reshape(home_rows, query_heads, HEAD_SIZE)
    attended = narrow_rows(combined / weight_sum[..., None]).reshape(
        home_rows, query_heads * HEAD_SIZE
    )
    projected = lax.psum(jnp.dot(attended, wo, preferred_element_type=jnp.float32), "kv")
    residual = narrow_rows(hidden.astype(jnp.float32) + projected)
    mlp_in = rms_scale(residual, norm_mlp)
    columns = lax.all_to_all(mlp_in, "pool", split_axis=1, concat_axis=0, tiled=True)
    hidden_width = w_gate.shape[1]
    gate_term = jnp.dot(columns, w_gate, preferred_element_type=jnp.float32)
    up_term = jnp.dot(columns, w_up, preferred_element_type=jnp.float32)
    summed = lax.psum_scatter(
        jnp.concatenate([gate_term, up_term], axis=1), "pool", scatter_dimension=0, tiled=True
    )
    activation = narrow_rows(jax.nn.silu(summed[:, :hidden_width]) * summed[:, hidden_width:])
    projected_down = jnp.dot(
        lax.all_gather(activation, "pool", axis=0, tiled=True),
        w_down,
        preferred_element_type=jnp.float32,
    )
    mlp_out = narrow_rows(lax.psum(projected_down, "kv"))
    returned = lax.all_to_all(mlp_out, "pool", split_axis=0, concat_axis=1, tiled=True)
    return (residual.astype(jnp.float32) + returned.astype(jnp.float32)).astype(jnp.bfloat16)


def solution(mesh):
    return jax.shard_map(
        per_device,
        mesh=mesh,
        in_specs=(
            P("pool", None),
            P(),
            P(None, "kv"),
            P(None, None, "kv"),
            P("kv", None),
            P(None, "pool", None, "kv"),
            P("pool"),
            P(),
            P(),
            P("pool", "kv"),
            P("pool", "kv"),
            P("kv", "pool"),
        ),
        out_specs=P("pool", None),
        check_vma=False,
    )
```

profile of v0, /device:TPU:1, one launch (start us, length us, event | category | flops | bytes accessed | tf_op | source)
XLA Modules:
  0.0 791.9 jit_solution(5610471597167837660)
XLA Ops:
  8.0 1.2 dynamic_slice.42
  10.6 1.3 multiply_reduce_fusion.1
  13.3 1.5 fusion.5
  15.0 70.3 %all-gather.3 = bf16[64,1,256]{2,1,0:T(2,128)(2,1)S(1)} all-gather(bf16[1,1,256]{2,1,0:T(2,128)(2,1)S(1)} %reshape.618), channel_id=1, replica_groups=mesh['kv'=8,'pool'=64] {'pool'}, dimensions={0}, use_global_device_ids=true | all-gather | bytes 33280 | tf_op jit(solution)/shard_map/all_gather | solution.py:88
  85.5 1.3 gather_fusion
  87.6 1.5 fusion.61
  89.6 1.3 fusion.10
  90.9 0.9 fusion.20
  91.9 1.2 convolution_bitcast_fusion.2
  93.3 1.2 fusion.4
  94.7 62.4 %all-gather.5 = f32[64,64,2]{1,2,0:T(2,128)S(1)} all-gather(f32[1,64,2]{1,2,0:T(2,128)S(1)} %convolution_bitcast_fusion), channel_id=3, replica_groups=mesh['kv'=8,'pool'=64] {'pool'}, dimensions={0}, use_global_device_ids=true | all-gather | bytes 33280 | tf_op jit(solution)/shard_map/all_gather | solution.py:19
  157.2 67.8 %all-gather.4 = f32[64,64,2]{1,2,0:T(2,128)S(1)} all-gather(f32[1,64,2]{1,2,0:T(2,128)S(1)} %bitcast.156), channel_id=2, replica_groups=mesh['kv'=8,'pool'=64] {'pool'}, dimensions={0}, use_global_device_ids=true | all-gather | bytes 33280 | tf_op jit(solution)/shard_map/all_gather | solution.py:19
  225.2 18.5 %all-gather.9.cloned.1.call-done = f32[4096,256]{1,0:T(8,128)} async-done(((f32[64,256]{1,0:T(8,128)}), f32[4096,256]{1,0:T(8,128)}) %all-gather.9.cloned.1.call-update) | async-done | bytes 4194320 | tf_op jit(solution)/shard_map/all_gather | solution.py:19
  244.6 87.2 %while.19 = (s32[]{:T(128)}, f32[64,2]{0,1:T(2,128)S(1)}, f32[64,2]{0,1:T(2,128)S(1)}, f32[64,256]{1,0:T(8,128)S(1)}, f32[64,64,2]{1,2,0:T(2,128)S(1)}, /*index=...) while((s32[]{:T(128)}, f32[64,2]{0,1:T(2,128)S(1)}, ...), condition=%wide.region_6.7_spmd, body=%wide.region_5.6_spmd.sunk | while | flops 49925 | bytes 466071 | solution.py:25
  245.0 0.9 fusion.74
  249.2 0.9 fusion.74
  250.6 0.9 fusion.74
  252.0 0.9 fusion.74
  253.3 0.9 fusion.74
  258.9 0.9 fusion.74
  260.3 0.9 fusion.74
  261.7 0.9 fusion.74
  267.2 0.9 fusion.74
  268.6 0.9 fusion.74
  332.4 43.6 %psum.14 = f32[1,2048]{1,0:T(1,128)S(1)} all-reduce(f32[1,2048]{1,0:T(1,128)S(1)} %fusion.62), channel_id=1, replica_groups=mesh['kv'=8,'pool'=64] {'kv'}, use_global_device_ids=true, to_apply=%region_8.9 | all-reduce | flops 2048 | bytes 16384 | tf_op jit(solution)/shard_map/psum | solution.py:151
  377.5 22.5 %all_to_all.30 = bf16[1,64,32]{2,0,1:T(2,128)(2,1)S(1)} all-to-all(bf16[1,64,32]{2,0,1:T(2,128)(2,1)S(1)} %all_to_all.27), channel_id=1, replica_groups=mesh['kv'=8,'pool'=64] {'pool'}, dimensions={1} | all-to-all | bytes 8192 | tf_op jit(solution)/shard_map/all_to_all | solution.py:154
  401.4 1.3 dynamic-slice
  402.7 247.1 %all-reduce.3.cloned.1.call-done = f32[64,2048]{1,0:T(8,128)} async-done(((f32[64,2048]{1,0:T(8,128)}), f32[64,2048]{1,0:T(8,128)}) %all-reduce.3.cloned.1.call-update) | async-done | bytes 524304
  649.8 1.5 fusion.39
  651.3 60.4 %all-gather.6 = bf16[64,1,1024]{2,1,0:T(2,128)(2,1)S(1)} all-gather(bf16[1,1,1024]{2,1,0:T(2,128)(2,1)S(1)} %bitcast.153), channel_id=1, replica_groups=mesh['kv'=8,'pool'=64] {'pool'}, dimensions={0}, use_global_device_ids=true | all-gather | bytes 133120 | tf_op jit(solution)/shard_map/all_gather | solution.py:163
  711.9 49.9 %psum.15 = bf16[64,32]{0,1:T(8,128)(2,1)S(1)} all-reduce(f32[64,32]{0,1:T(8,128)S(1)} %fusion.17), channel_id=1, replica_groups=mesh['kv'=8,'pool'=64] {'kv'}, use_global_device_ids=true, to_apply=%region_11.12 | all-reduce | flops 2048 | bytes 12288 | tf_op jit(solution)/shard_map/psum | solution.py:167
  761.9 22.4 %all_to_all.31 = bf16[64,1,32]{2,1,0:T(2,128)(2,1)S(1)} all-to-all(bf16[64,1,32]{2,1,0:T(2,128)(2,1)S(1)} %copy.51), channel_id=1, replica_groups=mesh['kv'=8,'pool'=64] {'pool'}, dimensions={0} | all-to-all | bytes 8192 | tf_op jit(solution)/shard_map/all_to_all | solution.py:168
  (435 shorter events, 85.8 us)
Async XLA Ops:
  6.5 325.6 %copy-start = (bf16[256,2048]{1,0:T(8,128)(2,1)S(1)}, bf16[256,2048]{1,0:T(8,128)(2,1)}, u32[]{:S(2)}) copy-start(bf16[256,2048]{1,0:T(8,128)(2,1)} %param.18) | copy-start | bytes 3145732
  6.5 88.0 %copy-start.4 = (bf16[2048]{0:T(1024)(128)(2,1)S(1)}, bf16[2048]{0:T(1024)(128)(2,1)}, u32[]{:S(2)}) copy-start(bf16[2048]{0:T(1024)(128)(2,1)} %param.22) | copy-start | bytes 12292
  6.5 237.2 %all-gather.9.cloned.1.call-start = ((), (), s32[]{:S(2)}) async-start(), calls=%async_computation.2 | async-start | bytes 4259840 | tf_op jit(solution)/shard_map/all_gather | solution.py:19
  14.8 361.2 %copy-start.1 = (bf16[1,2048]{1,0:T(2,128)(2,1)S(1)}, bf16[1,2048]{1,0:T(2,128)(2,1)}, u32[]{:S(2)}) copy-start(bf16[1,2048]{1,0:T(2,128)(2,1)} %param.14) | copy-start | bytes 12292
  15.0 385.1 %copy-start.2 = (bf16[32,1024]{1,0:T(8,128)(2,1)S(1)}, bf16[32,1024]{1,0:T(8,128)(2,1)}, u32[]{:S(2)}) copy-start(bf16[32,1024]{1,0:T(8,128)(2,1)} %param.24) | copy-start | bytes 196612
  85.5 314.8 %copy-start.3 = (bf16[32,1024]{1,0:T(8,128)(2,1)S(1)}, bf16[32,1024]{1,0:T(8,128)(2,1)}, u32[]{:S(2)}) copy-start(bf16[32,1024]{1,0:T(8,128)(2,1)} %param.23) | copy-start | bytes 196612
  91.8 558.0 %all-reduce.3.cloned.1.call-start = ((), (), s32[]{:S(2)}) async-start(), calls=%async_computation.3 | async-start | bytes 1048576
  93.1 618.6 %copy-start.5 = (bf16[1024,32]{0,1:T(8,128)(2,1)S(1)}, bf16[1024,32]{0,1:T(8,128)(2,1)}, u32[]{:S(2)}) copy-start(bf16[1024,32]{0,1:T(8,128)(2,1)} %param.25) | copy-start | bytes 196612
Sparse Core Ops, SparseCore 0:
  92.0 151.7 all-gather.8
  401.5 248.2 all-reduce.2
where the time goes:
time: 798 us; the launch traced here: 792 us
  blocking collectives  399 us (50%)
  waiting for transfers between devices  266 us (33%)
  other arithmetic  66.5 us (8%)
  local copies, waits for them, and re-layouts  33.7 us (4%)
  between operations  15.6 us (2%)
  matrix products  8.64 us (1%)
    unnamed x3, waiting for transfers between devices  247 us
    all_gather x2, blocking collectives, combined_all(): everything = jax.tree.map(lambda part: lax.all_gather(part, axis), x)  130 us
    all_gather x1, blocking collectives, per_device(): lax.all_gather(query_rows.reshape(home_rows, query_heads * HEAD_SIZE), 'p...  70.3 us
    all_gather x1, blocking collectives, per_device(): lax.all_gather(activation, 'pool', axis=0, tiled=True)  60.4 us
    add x63, other arithmetic, combine(): early_out + late_out  55.6 us
    psum x1, blocking collectives, per_device(): mlp_out = narrow_rows(lax.psum(projected_down, 'kv'))  49.9 us
    psum x1, blocking collectives, per_device(): lax.psum(jnp.dot(attended, wo, preferred_element_type=jnp.float32), 'kv')  43.6 us
    all_to_all x1, blocking collectives, per_device(): lax.all_to_all(mlp_in, 'pool', split_axis=1, concat_axis=0, tiled=True)  22.5 us
  transfers between devices with their start and end apart: 2, of which 2 were waited for; matrix products, arithmetic and copies ran while one was open for 1% of the time, Pallas kernels for 0%

commit v1 on v0

--- a/solution.py
+++ b/solution.py
@@ -13,16 +13,6 @@
 NEGATIVE = -1e30
 EPSILON = 1e-05
 ROPE_BASE = 1000000.0
-
-
-def combined_all(x, axis, combine):
-    everything = jax.tree.map(lambda part: lax.all_gather(part, axis), x)
-    initial = jax.tree.map(lambda part: part[0], everything)
-
-    def step(k, so_far):
-        return combine(so_far, jax.tree.map(lambda part: part[k], everything))
-
-    return lax.fori_loop(1, lax.axis_size(axis), step, initial)
 
 
 def narrow_rows(tensor):
@@ -49,18 +39,6 @@
     return jnp.concatenate(
         [leading * cosine - trailing * sine_of, trailing * cosine + leading * sine_of], axis=-1
     )
-
-
-def combine(earlier, latter):
-    highest = jnp.maximum(earlier[0], latter[0])
-    scale_early = jnp.exp(earlier[0] - highest)
-    scale_late = jnp.exp(latter[0] - highest)
-    row_count, head_count = highest.shape
-    feature = earlier[2].shape[1] // head_count
-    early_out = earlier[2].reshape(row_count, head_count, feature) * scale_early[:, :, None]
-    late_out = latter[2].reshape(row_count, head_count, feature) * scale_late[:, :, None]
-    weight_sum = earlier[1] * scale_early + latter[1] * scale_late
-    return (highest, weight_sum, (early_out + late_out).reshape(row_count, head_count * feature))
 
 
 def per_device(
@@ -95,39 +73,34 @@
     live_slot = slot_entry >= 0
     owners = jnp.where(live_slot, slot_entry // max_blocks, 0)
     block_index = jnp.where(live_slot, slot_entry % max_blocks, 0)
-    picked = every_query[owners]
-    block_keys = cache[0].reshape(slot_count, block_len, shared_heads, HEAD_SIZE)
-    block_values = cache[1].reshape(slot_count, block_len, shared_heads, HEAD_SIZE)
-    scores = jnp.einsum("sgjd,stgd->sgjt", picked, block_keys, preferred_element_type=jnp.float32)
     position = block_index[:, None] * block_len + jnp.arange(block_len, dtype=jnp.int32)[None, :]
     in_range = live_slot[:, None] & (position < lengths[owners][:, None])
-    scores = jnp.where(in_range[:, None, None, :], scores, NEGATIVE)
-    block_max = jnp.max(scores, axis=-1)
-    same_owner = (owners[:, None] == owners[None, :]) & live_slot[:, None] & live_slot[None, :]
-    holder_max = jnp.max(jnp.where(same_owner[:, :, None, None], block_max[None], NEGATIVE), axis=1)
-    raised = jnp.where(in_range[:, None, None, :], jnp.exp(scores - holder_max[..., None]), 0.0)
-    holder_total = jnp.sum(raised, axis=-1)
-    holder_output = jnp.einsum(
-        "sgjt,stgd->sgjd", narrow_rows(raised), block_values, preferred_element_type=jnp.float32
+    token_owner = jnp.where(in_range, owners[:, None], -1).reshape(1, slot_count * block_len)
+    keys = cache[0].reshape(slot_count * block_len, HEAD_SIZE)
+    values = cache[1].reshape(slot_count * block_len, HEAD_SIZE)
+    stacked = every_query.reshape(request_list, query_heads, HEAD_SIZE).transpose(1, 0, 2)
+    stacked = stacked.reshape(query_heads * request_list, HEAD_SIZE)
+    scores = lax.dot_general(
+        stacked, keys, (((1,), (1,)), ((), ())), preferred_element_type=jnp.float32
     )
-    member = (owners[:, None] == jnp.arange(request_list, dtype=jnp.int32)[None, :]) & live_slot[
-        :, None
-    ]
-    request_max = jnp.max(jnp.where(member.T[:, :, None, None], holder_max[None], NEGATIVE), axis=1)
-    request_max = request_max.reshape(request_list, query_heads)
-    member_float = member.astype(jnp.float32)
-    request_total = jnp.einsum(
-        "sr,sgj->rgj", member_float, holder_total, precision=lax.Precision.HIGHEST
-    )
-    request_total = request_total.reshape(request_list, query_heads)
-    request_out = jnp.einsum(
-        "sr,sgjd->rgjd", member_float, holder_output, precision=lax.Precision.HIGHEST
-    )
-    request_out = request_out.reshape(request_list, query_heads * HEAD_SIZE)
-    merged = combined_all((request_max, request_total, request_out), "pool", combine)
-    part_max = lax.dynamic_slice_in_dim(merged[0], home_index * home_rows, home_rows)
-    part_total = lax.dynamic_slice_in_dim(merged[1], home_index * home_rows, home_rows)
-    part_out = lax.dynamic_slice_in_dim(merged[2], home_index * home_rows, home_rows)
+    row_owner = jnp.tile(jnp.arange(request_list, dtype=jnp.int32), query_heads)[:, None]
+    taken = row_owner == token_owner
+    scores = jnp.where(taken, scores, NEGATIVE)
+    row_max = jnp.max(scores, axis=-1, keepdims=True)
+    raised = jnp.where(taken, jnp.exp(scores - row_max), 0.0)
+    row_total = jnp.sum(raised, axis=-1, keepdims=True)
+    row_out = jnp.dot(raised.astype(jnp.bfloat16), values, preferred_element_type=jnp.float32)
+    packed = jnp.concatenate(
+        [row_out, jnp.broadcast_to(row_max, (row_max.shape[0], 64)),
+         jnp.broadcast_to(row_total, (row_max.shape[0], 64))], axis=1
+    ).reshape(query_heads, request_list, 256).transpose(1, 0, 2).reshape(request_list, query_heads * 256)
+    arrived = lax.all_to_all(packed, "pool", split_axis=0, concat_axis=0, tiled=True)
+    arrived = arrived.reshape(request_list, query_heads, 256)
+    every_max = arrived[:, :, 128]
+    part_max = jnp.max(every_max, axis=0, keepdims=True)
+    factor = jnp.exp(every_max - part_max)
+    part_total = jnp.sum(factor * arrived[:, :, 192], axis=0, keepdims=True)
+    part_out = jnp.sum(factor[:, :, None] * arrived[:, :, :128], axis=0).reshape(1, query_heads * HEAD_SIZE)
     own_query = query_rows.reshape(home_rows, shared_heads, queries_per_shared, HEAD_SIZE).astype(
         jnp.float32
     )
@@ -155,8 +128,11 @@
     hidden_width = w_gate.shape[1]
     gate_term = jnp.dot(columns, w_gate, preferred_element_type=jnp.float32)
     up_term = jnp.dot(columns, w_up, preferred_element_type=jnp.float32)
-    summed = lax.psum_scatter(
-        jnp.concatenate([gate_term, up_term], axis=1), "pool", scatter_dimension=0, tiled=True
+    sent = jnp.concatenate([gate_term, up_term], axis=1).astype(jnp.bfloat16)
+    summed = jnp.sum(
+        lax.all_to_all(sent, "pool", split_axis=0, concat_axis=0, tiled=True).astype(jnp.float32),
+        axis=0,
+        keepdims=True,
     )
     activation = narrow_rows(jax.nn.silu(summed[:, :hidden_width]) * summed[:, hidden_width:])
     projected_down = jnp.dot(

time: 798 us -> 312 us (0.39)
  waiting for transfers between devices: 266 us -> 12.6 us
  blocking collectives: 399 us -> 269 us
  other arithmetic: 66.5 us -> 5.5 us
  local copies, waits for them, and re-layouts: 33.7 us -> 6.74 us
  between operations: 15.6 us -> 2.35 us
  starting transfers between devices: 0.04 us -> 9.45 us
    unnamed x3 -> x0, waiting for transfers between devices: 247 us -> none
    all_gather x2 -> x0, blocking collectives: 130 us -> none  [combined_all(): everything = jax.tree.map(lambda part: lax.all_gather(part, axis), x)]
    add x126 -> x1, other arithmetic: 57.2 us -> 0.01 us  [per_device(): weight_sum = part_total * old_scale + new_scale]
    all_to_all x0 -> x1, blocking collectives: none -> 22 us  [per_device(): lax.all_to_all(sent, 'pool', split_axis=0, concat_axis=0, tiled=True)]
    all_gather x1 -> x0, waiting for transfers between devices: 18.5 us -> none  [combined_all(): everything = jax.tree.map(lambda part: lax.all_gather(part, axis), x)]
    mul x126 -> x1, local copies, waits for them, and re-layouts: 15.6 us -> 0.1 us  [per_device(): factor[:, :, None] * arrived[:, :, :128]]
    all_to_all x0 -> x1, waiting for transfers between devices: none -> 12.6 us  [per_device(): lax.all_to_all(packed, 'pool', split_axis=0, concat_axis=0, tiled=True)]
    exp x126 -> x0, local copies, waits for them, and re-layouts: 12.1 us -> none  [the longest x63 6.07 us: combine(): scale_early = jnp.exp(earlier[0] - highest)]
  transfers between devices with their start and end apart: 2 -> 1, of which waited for: 2 -> 1; matrix products, arithmetic and copies ran while one was open for 1% -> 0% of each run, Pallas kernels for 0% -> 0%
where the time goes in v1:
time: 312 us; the launch traced here: 309 us
  blocking collectives  269 us (86%)
  waiting for transfers between devices  12.6 us (4%)
  starting transfers between devices  9.45 us (3%)
  local copies, waits for them, and re-layouts  6.74 us (2%)
  other arithmetic  5.5 us (2%)
  matrix products  3.47 us (1%)
    all_gather x1, blocking collectives, per_device(): lax.all_gather(query_rows.reshape(home_rows, query_heads * HEAD_SIZE), 'p...  70.2 us
    all_gather x1, blocking collectives, per_device(): lax.all_gather(activation, 'pool', axis=0, tiled=True)  62.7 us
    psum x1, blocking collectives, per_device(): mlp_out = narrow_rows(lax.psum(projected_down, 'kv'))  42.9 us
    psum x1, blocking collectives, per_device(): lax.psum(jnp.dot(attended, wo, preferred_element_type=jnp.float32), 'kv')  33.6 us
    all_to_all x1, blocking collectives, per_device(): lax.all_to_all(sent, 'pool', split_axis=0, concat_axis=0, tiled=True)  22 us
    all_to_all x1, blocking collectives, per_device(): lax.all_to_all(mlp_out, 'pool', split_axis=0, concat_axis=1, tiled=True)  19 us
    all_to_all x1, blocking collectives, per_device(): lax.all_to_all(mlp_in, 'pool', split_axis=1, concat_axis=0, tiled=True)  18.3 us
    all_to_all x1, waiting for transfers between devices, per_device(): lax.all_to_all(packed, 'pool', split_axis=0, concat_axis=0, tiled=True)  12.6 us
  transfers between devices with their start and end apart: 1, of which 1 were waited for; matrix products, arithmetic and copies ran while one was open for 0% of the time, Pallas kernels for 0%

profile of v1, /device:TPU:1, one launch (start us, length us, event | category | flops | bytes accessed | tf_op | source)
XLA Modules:
  0.0 308.8 jit_solution(4484563222303054181)
XLA Ops:
  0.0 0.7 copy-done.9
  0.8 0.6 copy-done.1
  1.5 0.6 dynamic_slice.3
  2.8 0.6 multiply_reduce_fusion.1
  4.1 1.5 fusion.4
  5.7 70.2 %all-gather = bf16[64,1,256]{2,1,0:T(2,128)(2,1)S(1)} all-gather(bf16[1,1,256]{2,1,0:T(2,128)(2,1)S(1)} %reshape.500), channel_id=1, replica_groups=mesh['kv'=8,'pool'=64] {'pool'}, dimensions={0}, use_global_device_ids=true | all-gather | bytes 33280 | tf_op jit(solution)/shard_map/all_gather | solution.py:66
  76.2 0.7 gather_fusion
  77.1 0.4 fusion.52
  77.5 0.4 fusion.7
  77.9 0.4 fusion.9
  78.6 0.8 all_to_all.40
  79.4 9.5 %all-to-all-start = ((f32[64,1,512]{2,1,0:T(1,128)}), f32[64,1,512]{2,1,0:T(1,128)S(1)}, u32[]{:S(2)}, u32[]{:S(2)}) async-start(f32[64,1,512]{2,1,0:T(1,128)} %all_to_all.40), calls=%async_computation | async-start | bytes 262144 | tf_op jit(solution)/shard_map/all_to_all | solution.py:97
  89.4 0.5 copy-done.8
  90.1 12.6 %all-to-all-done = f32[64,1,512]{2,1,0:T(1,128)S(1)} async-done(((f32[64,1,512]{2,1,0:T(1,128)}), f32[64,1,512]{2,1,0:T(1,128)S(1)}, u32[]{:S(2)}, u32[]{:S(2)}) %all-to-all-start) | async-done | bytes 131104 | tf_op jit(solution)/shard_map/all_to_all | solution.py:97
  102.7 0.3 reduce.7
  103.1 0.2 fusion.51
  104.1 0.2 fusion.53
  104.4 33.6 %psum.14 = f32[1,2048]{1,0:T(1,128)S(1)} all-reduce(f32[1,2048]{1,0:T(1,128)S(1)} %fusion.53), channel_id=1, replica_groups=mesh['kv'=8,'pool'=64] {'kv'}, use_global_device_ids=true, to_apply=%region_7.8 | all-reduce | flops 2048 | bytes 16384 | tf_op jit(solution)/shard_map/psum | solution.py:124
  138.0 0.6 multiply_reduce_fusion
  139.5 18.3 %all_to_all.46 = bf16[1,64,32]{2,0,1:T(2,128)(2,1)S(1)} all-to-all(bf16[1,64,32]{2,0,1:T(2,128)(2,1)S(1)} %all_to_all.41), channel_id=1, replica_groups=mesh['kv'=8,'pool'=64] {'pool'}, dimensions={1} | all-to-all | bytes 8192 | tf_op jit(solution)/shard_map/all_to_all | solution.py:127
  157.9 0.2 fusion
  158.1 0.6 copy-done.6
  158.7 0.2 fusion.1
  159.0 0.5 broadcast.240
  159.5 0.8 reduce.13
  160.4 22.0 %all_to_all.47 = bf16[64,2,1024]{2,1,0:T(2,128)(2,1)S(1)} all-to-all(bf16[64,2,1024]{2,1,0:T(2,128)(2,1)S(1)} %reshape.527), channel_id=1, replica_groups=mesh['kv'=8,'pool'=64] {'pool'}, dimensions={0} | all-to-all | bytes 524288 | tf_op jit(solution)/shard_map/all_to_all | solution.py:133
  182.4 0.2 reshape.528
  182.6 0.5 convert_reduce_fusion
  183.2 62.7 %all-gather.1 = bf16[64,1,1024]{2,1,0:T(2,128)(2,1)S(1)} all-gather(bf16[1,1,1024]{2,1,0:T(2,128)(2,1)S(1)} %bitcast.109), channel_id=1, replica_groups=mesh['kv'=8,'pool'=64] {'pool'}, dimensions={0}, use_global_device_ids=true | all-gather | bytes 133120 | tf_op jit(solution)/shard_map/all_gather | solution.py:139
  246.0 42.9 %psum.15 = bf16[64,32]{0,1:T(8,128)(2,1)S(1)} all-reduce(f32[64,32]{0,1:T(8,128)S(1)} %fusion.19), channel_id=1, replica_groups=mesh['kv'=8,'pool'=64] {'kv'}, use_global_device_ids=true, to_apply=%region_10.11 | all-reduce | flops 2048 | bytes 12288 | tf_op jit(solution)/shard_map/psum | solution.py:143
  289.0 19.0 %all_to_all.48 = bf16[64,1,32]{2,1,0:T(2,128)(2,1)S(1)} all-to-all(bf16[64,1,32]{2,1,0:T(2,128)(2,1)S(1)} %copy.54), channel_id=1, replica_groups=mesh['kv'=8,'pool'=64] {'pool'}, dimensions={0} | all-to-all | bytes 8192 | tf_op jit(solution)/shard_map/all_to_all | solution.py:144
  308.2 0.6 add_convert_fusion
  (69 shorter events, 3.4 us)
Async XLA Ops:
  0.0 104.1 %copy-start = (bf16[256,2048]{1,0:T(8,128)(2,1)S(1)}, bf16[256,2048]{1,0:T(8,128)(2,1)}, u32[]{:S(2)}) copy-start(bf16[256,2048]{1,0:T(8,128)(2,1)} %param.16) | copy-start | bytes 3145732
  0.0 0.7 copy-start.9
  0.7 2.0 copy-start.7
  0.8 2.0 copy-start.4
  0.8 0.7 copy-start.1
  0.8 76.1 %copy-start.3 = (bf16[2,16,128,128]{3,2,1,0:T(8,128)(2,1)S(1)}, bf16[2,16,128,128]{3,2,1,0:T(8,128)(2,1)}, u32[]{:S(2)}) copy-start(bf16[2,16,128,128]{3,2,1,0:T(8,128)(2,1)} %param.17) | copy-start | bytes 3145732
  78.3 10.6 %copy-start.2 = (bf16[2,2048,128]{2,1,0:T(8,128)(2,1)S(1)}, bf16[2,2048,128]{2,1,0:T(8,128)(2,1)}, u32[]{:S(2)}) copy-start(bf16[2,2048,128]{2,1,0:T(8,128)(2,1)} %param.15) | copy-start | bytes 3145732
  79.4 23.3 %all-to-all-start = ((f32[64,1,512]{2,1,0:T(1,128)}), f32[64,1,512]{2,1,0:T(1,128)S(1)}, u32[]{:S(2)}, u32[]{:S(2)}) async-start(f32[64,1,512]{2,1,0:T(1,128)} %all_to_all.40), calls=%async_computation | async-start | bytes 262144 | tf_op jit(solution)/shard_map/all_to_all | solution.py:97
  89.2 0.7 copy-start.8
  139.4 18.5 %copy-start.5 = (bf16[32,1024]{1,0:T(8,128)(2,1)S(1)}, bf16[32,1024]{1,0:T(8,128)(2,1)}, u32[]{:S(2)}) copy-start(bf16[32,1024]{1,0:T(8,128)(2,1)} %param.21) | copy-start | bytes 196612
  157.9 0.9 copy-start.6
  183.2 62.7 %copy-start.10 = (bf16[1024,32]{0,1:T(8,128)(2,1)S(1)}, bf16[1024,32]{0,1:T(8,128)(2,1)}, u32[]{:S(2)}) copy-start(bf16[1024,32]{0,1:T(8,128)(2,1)} %param.23) | copy-start | bytes 196612

commit v2 on v1

v2 whole, which is shorter than its diff:
```python
import functools
import math

import jax
import jax.numpy as jnp
from jax import lax
from jax.experimental import pallas as pl
from jax.experimental.pallas import tpu as pltpu
from jax.sharding import PartitionSpec as P

HEAD_SIZE = 128
LANES = 128
NEGATIVE = -1e30
EPSILON = 1e-05
ROPE_BASE = 1000000.0
MESH = pl.DeviceIdType.MESH
F32 = jnp.float32
BF16 = jnp.bfloat16


def rounded(x):
    return x.astype(BF16).astype(F32)


def rms(x, gain):
    mean_square = jnp.mean(x * x, axis=-1, keepdims=True)
    return (x * lax.rsqrt(mean_square + EPSILON) * gain).astype(BF16)


def layer_kernel(
    pool, kv,
    hidden, norm_attn, wq, wkv, wo, cache, owner, cosine, sine, norm_mlp, w_gate, w_up, w_down,
    out,
    wide, gate_pad, up_pad, down_pad,
    q_send, q_recv, part_send, part_recv, proj_send, proj_recv, in_send, in_recv,
    gu_send, gu_recv, act_send, act_recv, down_send, down_recv, fin_send, fin_recv,
    send_sem, recv_sem,
):
    me = lax.axis_index("pool")
    my_kv = lax.axis_index("kv")
    quarter = lax.rem(me, 4)

    barrier = pltpu.get_barrier_semaphore()

    def greet_pool(k, carry):
        pl.semaphore_signal(
            barrier, inc=1, device_id={"pool": lax.rem(me + k, pool)}, device_id_type=MESH
        )
        return carry

    def greet_kv(k, carry):
        pl.semaphore_signal(
            barrier, inc=1, device_id={"kv": lax.rem(my_kv + k, kv)}, device_id_type=MESH
        )
        return carry

    lax.fori_loop(1, pool, greet_pool, 0)
    lax.fori_loop(1, kv, greet_kv, 0)

    def scatter(phase, source_of, target, axis, count, mine):
        def body(k, carry):
            peer = lax.rem(mine + k, count)
            pltpu.make_async_remote_copy(
                src_ref=source_of(peer),
                dst_ref=target.at[mine],
                send_sem=send_sem.at[phase],
                recv_sem=recv_sem.at[phase],
                device_id={axis: peer},
                device_id_type=MESH,
            ).start()
            return carry

        lax.fori_loop(1, count, body, 0)

    def arrive(phase, target, count):
        view = target.at[pl.ds(0, count - 1)]
        pltpu.make_async_copy(view, view, recv_sem.at[phase]).wait()

    def sent(phase, target, count):
        view = target.at[pl.ds(0, count - 1)]
        pltpu.make_async_copy(view, view, send_sem.at[phase]).wait()

    normed = rms(hidden[...].astype(F32), norm_attn[...].astype(F32))
    cos_row = cosine[...]
    sin_row = sine[...]

    def rotated(v):
        return v * cos_row + pltpu.roll(v, HEAD_SIZE // 2, 1) * sin_row

    q = jnp.dot(normed, wq[...], preferred_element_type=F32)
    scale = HEAD_SIZE ** (-0.5)
    q0 = rounded(rotated(q[:, :128]) * scale)
    q1 = rounded(rotated(q[:, 128:]) * scale)
    new_key = rounded(rotated(jnp.dot(normed, wkv[0], preferred_element_type=F32)))
    new_value = rounded(jnp.dot(normed, wkv[1], preferred_element_type=F32))
    own_q = jnp.concatenate([q0, q1], axis=1)
    q_send[0] = own_q
    q_recv[me] = own_q

    pl.semaphore_wait(barrier, pool - 1 + kv - 1)
    scatter(0, lambda peer: q_send.at[0], q_recv, "pool", pool, me)

    for g in range(4):
        here = quarter == g
        gate_pad[pl.ds(32 * g, 32), :] = jnp.where(here, w_gate[...].astype(F32), 0.0).astype(BF16)
        up_pad[pl.ds(32 * g, 32), :] = jnp.where(here, w_up[...].astype(F32), 0.0).astype(BF16)
    place = (
        lax.broadcasted_iota(jnp.int32, (32, LANES), 1)
        == lax.broadcasted_iota(jnp.int32, (32, LANES), 0) + 32 * quarter
    )
    down_pad[...] = jnp.dot(
        w_down[...], jnp.where(place, 1.0, 0.0).astype(BF16), preferred_element_type=F32
    ).astype(BF16)

    arrive(0, q_recv, pool)
    every = q_recv[:, 0, :]
    rows = jnp.concatenate([every[:, :128], every[:, 128:]], axis=0).astype(BF16)
    tokens = cache.shape[1]
    scores = lax.dot_general(rows, cache[0], (((1,), (1,)), ((), ())), preferred_element_type=F32)
    row_owner = lax.rem(lax.broadcasted_iota(jnp.int32, (2 * pool, 1), 0), pool)
    taken = row_owner == owner[...]
    scores = jnp.where(taken, scores, NEGATIVE)
    row_max = jnp.max(scores, axis=1, keepdims=True)
    raised = jnp.where(taken, jnp.exp(scores - row_max), 0.0)
    row_total = jnp.sum(raised, axis=1, keepdims=True)
    row_out = jnp.dot(raised.astype(BF16), cache[1], preferred_element_type=F32)
    lane = lax.broadcasted_iota(jnp.int32, (pool, LANES), 1)
    stats = jnp.where(
        lane == 0,
        row_max[:pool],
        jnp.where(lane == 1, row_max[pool:], jnp.where(lane == 2, row_total[:pool], row_total[pool:])),
    )
    wide[:, 0:128] = row_out[:pool]
    wide[:, 128:256] = row_out[pool:]
    wide[:, 256:384] = stats

    def spread(target, width):
        def body(b, carry):
            block = wide[pl.ds(pl.multiple_of(b * 8, 8), 8), 0:width]
            for i in range(8):
                target[b * 8 + i] = block[i : i + 1]
            return carry

        lax.fori_loop(0, pool // 8, body, 0)

    spread(part_send, 384)
    part_recv[me] = part_send[me]
    scatter(1, lambda peer: part_send.at[peer], part_recv, "pool", pool, me)

    arrive(1, part_recv, pool)
    parts = part_recv[:, 0, :]
    heads = []
    for j, qj in ((0, q0), (1, q1)):
        maxima = parts[:, 256 + j : 257 + j]
        totals = parts[:, 258 + j : 259 + j]
        new_score = jnp.sum(qj * new_key, axis=1, keepdims=True)
        highest = jnp.maximum(jnp.max(maxima, axis=0, keepdims=True), new_score)
        factor = jnp.exp(maxima - highest)
        new_factor = jnp.exp(new_score - highest)
        weight = jnp.sum(totals * factor, axis=0, keepdims=True) + new_factor
        mixed = jnp.sum(parts[:, 128 * j : 128 * (j + 1)] * factor, axis=0, keepdims=True)
        heads.append((mixed + new_factor * new_value) / weight)
    attended = jnp.concatenate(heads, axis=1).astype(BF16)
    projected = jnp.dot(attended, wo[...], preferred_element_type=F32)
    proj_send[0] = projected
    proj_recv[my_kv] = projected
    scatter(2, lambda peer: proj_send.at[0], proj_recv, "kv", kv, my_kv)
    arrive(2, proj_recv, kv)
    total = proj_recv[0]
    for k in range(1, kv):
        total = total + proj_recv[k]
    residual = rounded(hidden[...].astype(F32) + total)
    mlp_in = rms(residual, norm_mlp[...].astype(F32)).astype(F32)
    groups = mlp_in.shape[1] // LANES
    for g in range(groups):
        in_send[g] = mlp_in[:, g * LANES : (g + 1) * LANES]
    in_recv[me] = in_send[me // 4]
    scatter(3, lambda peer: in_send.at[peer // 4], in_recv, "pool", pool, me)

    arrive(3, in_recv, pool)
    columns = in_recv[:, 0, :].astype(BF16)
    half = w_gate.shape[1]
    wide[:, 0:half] = jnp.dot(columns, gate_pad[...], preferred_element_type=F32)
    wide[:, half : 2 * half] = jnp.dot(columns, up_pad[...], preferred_element_type=F32)

    def spread_gu(b, carry):
        at = pl.ds(pl.multiple_of(b * 8, 8), 8)
        gate_rows = wide[at, 0:half]
        up_rows = wide[at, half : 2 * half]
        for i in range(8):
            both = jnp.concatenate([gate_rows[i : i + 1], up_rows[i : i + 1]], axis=0)
            gu_send[b * 8 + i] = both.astype(BF16)
        return carry

    lax.fori_loop(0, pool // 8, spread_gu, 0)
    gu_recv[me] = gu_send[me]
    scatter(4, lambda peer: gu_send.at[peer], gu_recv, "pool", pool, me)
    arrive(4, gu_recv, pool)
    summed = jnp.sum(gu_recv[...].astype(F32), axis=0)
    gate = summed[0:1]
    up = summed[1:2]
    activation = gate / (1.0 + jnp.exp(-gate)) * up
    act_row = rounded(activation)
    act_send[0] = act_row
    act_recv[me] = act_row
    scatter(5, lambda peer: act_send.at[0], act_recv, "pool", pool, me)

    arrive(5, act_recv, pool)
    activations = act_recv[:, 0, :].astype(BF16)
    wide[:, 0:LANES] = jnp.dot(activations, down_pad[...], preferred_element_type=F32)

    spread(down_send, LANES)
    down_recv[me] = down_send[me]
    scatter(6, lambda peer: down_send.at[peer], down_recv, "pool", pool, me)
    arrive(6, down_recv, pool)
    pieces = []
    for g in range(groups):
        piece = down_recv[4 * g]
        for j in range(1, 4):
            piece = piece + down_recv[4 * g + j]
        pieces.append(piece)
    down_row = jnp.concatenate(pieces, axis=1)
    fin_send[0] = down_row
    fin_recv[my_kv] = down_row
    scatter(7, lambda peer: fin_send.at[0], fin_recv, "kv", kv, my_kv)
    arrive(7, fin_recv, kv)
    total = fin_recv[0]
    for k in range(1, kv):
        total = total + fin_recv[k]
    out[...] = (residual + rounded(total)).astype(BF16)

    sent(0, q_recv, pool)
    sent(1, part_recv, pool)
    sent(2, proj_recv, kv)
    sent(3, in_recv, pool)
    sent(4, gu_recv, pool)
    sent(5, act_recv, pool)
    sent(6, down_recv, pool)
    sent(7, fin_recv, kv)


def per_device(
    hidden, norm_attn, wq, wkv, wo, cache, slot_entry, lengths, norm_mlp, w_gate, w_up, w_down,
    pool, kv,
):
    width = hidden.shape[1]
    half = w_gate.shape[1]
    home = lax.axis_index("pool")
    slot_count = slot_entry.shape[0]
    block_len = cache.shape[2]
    requests = lengths.shape[0]
    max_blocks = 64
    position = lax.dynamic_slice_in_dim(lengths, home, 1).astype(F32)
    halfway = HEAD_SIZE // 2
    frequency = jnp.exp(
        jnp.arange(halfway, dtype=F32) * (-2.0 * math.log(ROPE_BASE) / HEAD_SIZE)
    )
    angles = position[:, None] * frequency[None, :]
    cosine = jnp.cos(angles)
    sine = jnp.sin(angles)
    cosine = jnp.concatenate([cosine, cosine], axis=1)
    sine = jnp.concatenate([-sine, sine], axis=1)
    live = slot_entry >= 0
    owners = jnp.where(live, slot_entry // max_blocks, -1)
    blocks = jnp.where(live, slot_entry % max_blocks, 0)
    hit = owners[:, None] == jnp.arange(requests, dtype=jnp.int32)[None, :]
    extent = jnp.sum(jnp.where(hit, lengths[None, :], 0), axis=1)
    places = blocks[:, None] * block_len + jnp.arange(block_len, dtype=jnp.int32)[None, :]
    owner = jnp.where(places < extent[:, None], owners[:, None], -1)
    owner = owner.reshape(1, slot_count * block_len)
    vmem = pl.BlockSpec(memory_space=pltpu.VMEM)
    return pl.pallas_call(
        functools.partial(layer_kernel, pool, kv),
        out_shape=jax.ShapeDtypeStruct((1, width), BF16),
        in_specs=[vmem] * 13,
        out_specs=vmem,
        scratch_shapes=[
            pltpu.VMEM((pool, 2 * half), F32),
            pltpu.VMEM((LANES, half), BF16),
            pltpu.VMEM((LANES, half), BF16),
            pltpu.VMEM((half, LANES), BF16),
            pltpu.VMEM((1, 1, 256), F32),
            pltpu.VMEM((pool, 1, 256), F32),
            pltpu.VMEM((pool, 1, 384), F32),
            pltpu.VMEM((pool, 1, 384), F32),
            pltpu.VMEM((1, 1, width), F32),
            pltpu.VMEM((kv, 1, width), F32),
            pltpu.VMEM((width // LANES, 1, LANES), F32),
            pltpu.VMEM((pool, 1, LANES), F32),
            pltpu.VMEM((pool, 2, half), BF16),
            pltpu.VMEM((pool, 2, half), BF16),
            pltpu.VMEM((1, 1, half), F32),
            pltpu.VMEM((pool, 1, half), F32),
            pltpu.VMEM((pool, 1, LANES), F32),
            pltpu.VMEM((pool, 1, LANES), F32),
            pltpu.VMEM((1, 1, width), F32),
            pltpu.VMEM((kv, 1, width), F32),
            pltpu.SemaphoreType.DMA((8,)),
            pltpu.SemaphoreType.DMA((8,)),
        ],
        compiler_params=pltpu.CompilerParams(
            collective_id=0, has_side_effects=True, vmem_limit_bytes=48 * 1024 * 1024
        ),
    )(
        hidden, norm_attn.reshape(1, width), wq, wkv, wo,
        cache.reshape(2, slot_count * block_len, HEAD_SIZE), owner, cosine, sine,
        norm_mlp.reshape(1, width), w_gate, w_up, w_down,
    )


def solution(mesh):
    return jax.shard_map(
        functools.partial(per_device, pool=mesh.shape["pool"], kv=mesh.shape["kv"]),
        mesh=mesh,
        in_specs=(
            P("pool", None),
            P(),
            P(None, "kv"),
            P(None, None, "kv"),
            P("kv", None),
            P(None, "pool", None, "kv"),
            P("pool"),
            P(),
            P(),
            P("pool", "kv"),
            P("pool", "kv"),
            P("kv", "pool"),
        ),
        out_specs=P("pool", None),
        check_vma=False,
    )
```

time: 312 us -> 109 us (0.35)
  blocking collectives: 269 us -> 0 us
  Pallas kernels: 0 us -> 97.1 us
  waiting for transfers between devices: 12.6 us -> 0 us
  starting transfers between devices: 9.45 us -> 0 us
  other arithmetic: 5.5 us -> 1.84 us
  matrix products: 3.47 us -> 0 us
    all_gather x2 -> x0, blocking collectives: 133 us -> none  [the longest x1 70.2 us: per_device(): lax.all_gather(query_rows.reshape(home_rows, query_heads * HEAD_SIZE), 'p...]
    pallas_call x0 -> x1, Pallas kernels: none -> 97.1 us  [per_device(): pl.pallas_call(functools.partial(layer_kernel, pool, kv), out_shape=jax.S...]
    psum x2 -> x0, blocking collectives: 76.5 us -> none  [the longest x1 42.9 us: per_device(): mlp_out = narrow_rows(lax.psum(projected_down, 'kv'))]
    all_to_all x3 -> x0, blocking collectives: 59.3 us -> none  [the longest x1 22 us: per_device(): lax.all_to_all(sent, 'pool', split_axis=0, concat_axis=0, tiled=True)]
    all_to_all x1 -> x0, waiting for transfers between devices: 12.6 us -> none  [per_device(): lax.all_to_all(packed, 'pool', split_axis=0, concat_axis=0, tiled=True)]
    all_to_all x1 -> x0, starting transfers between devices: 9.45 us -> none  [per_device(): lax.all_to_all(packed, 'pool', split_axis=0, concat_axis=0, tiled=True)]
    dot_general x9 -> x0, matrix products: 3.47 us -> none  [the longest x1 1.47 us: per_device(): jnp.dot(normed_input, wq, preferred_element_type=jnp.float32)]
    unnamed x26 -> x18, local copies, waits for them, and re-layouts: 3.11 us -> 6.35 us
  transfers between devices with their start and end apart: 1 -> 0, of which waited for: 1 -> 0; matrix products, arithmetic and copies ran while one was open for 0% -> 0% of each run, Pallas kernels for 0% -> 0%
where the time goes in v2:
time: 109 us
  Pallas kernels  97.1 us (89%)
  local copies, waits for them, and re-layouts  9.01 us (8%)
  other arithmetic  1.84 us (2%)
    pallas_call x1, Pallas kernels, per_device(): pl.pallas_call(functools.partial(layer_kernel, pool, kv), out_shape=jax.S...  97.1 us
    unnamed x18, local copies, waits for them, and re-layouts  6.35 us

profile of v2, /device:TPU:1, one launch (start us, length us, event | category | flops | bytes accessed | tf_op | source)
XLA Modules:
  0.0 108.7 jit_solution(6907752559674006183)
XLA Ops:
  0.0 0.0 copy-start.7
  0.0 1.3 %dynamic_slice.3 = s32[1]{0:T(128)} dynamic-slice(s32[64]{0:T(128)} %param.19, s32[]{:T(128)S(6)} %select_n.47), dynamic_slice_sizes={1} | dynamic-slice | bytes 12 | tf_op jit(solution)/shard_map/dynamic_slice | solution.py:253
  1.9 0.1 fusion.4
  2.0 0.1 fusion.2
  2.0 0.1 pad_maximum_fusion.1.sine
  2.1 0.1 pad_maximum_fusion.cosine
  2.2 0.7 fusion.1
  2.9 0.8 select_reduce_fusion
  3.7 0.1 fusion
  3.8 0.7 reshape.95.norm_attn
  4.5 0.7 reshape.97.norm_mlp
  5.2 0.0 copy-done.7
  5.2 0.0 copy-start.4
  5.2 0.0 copy-start.5
  5.2 0.0 copy-start.6
  5.2 0.2 copy.14.w_down
  5.4 0.6 copy-done.4
  6.0 0.0 copy-done.5
  6.0 0.0 copy-done.6
  6.1 0.0 copy-start
  6.1 1.2 %copy-done = bf16[2048,256]{1,0:T(8,128)(2,1)S(1)} copy-done((bf16[2048,256]{1,0:T(8,128)(2,1)S(1)}, bf16[2048,256]{1,0:T(8,128)(2,1)}, u32[]{:S(2)}) %copy-start) | copy-done | bytes 1048600
  7.3 0.0 copy-start.1
  7.3 1.2 %copy-done.1 = bf16[2,2048,128]{2,1,0:T(8,128)(2,1)S(1)} copy-done((bf16[2,2048,128]{2,1,0:T(8,128)(2,1)S(1)}, bf16[2,2048,128]{2,1,0:T(8,128)(2,1)}, u32[]{:S(2)}) %copy-start.1) | copy-done | bytes 1048600
  8.5 0.0 copy-start.2
  8.5 1.2 %copy-done.2 = bf16[256,2048]{1,0:T(8,128)(2,1)S(1)} copy-done((bf16[256,2048]{1,0:T(8,128)(2,1)S(1)}, bf16[256,2048]{1,0:T(8,128)(2,1)}, u32[]{:S(2)}) %copy-start.2) | copy-done | bytes 1048600
  9.7 0.0 copy-start.3
  9.7 1.2 %copy-done.3 = bf16[2,16,128,128]{3,2,1,0:T(8,128)(2,1)S(1)} copy-done((bf16[2,16,128,128]{3,2,1,0:T(8,128)(2,1)S(1)}, bf16[2,16,128,128]{3,2,1,0:T(8,128)(2,1)}, u32[]{:S(2)}) %copy-start.3) | copy-done | bytes 1048600
  11.0 97.1 %shard_map.118 = bf16[1,2048]{1,0:T(2,128)(2,1)S(1)} custom-call(bf16[1,2048]{1,0:T(2,128)(2,1)S(1)} %copy-done.6, bf16[1,2048]{1,0:T(2,128)(2,1)S(1)} %reshape.95.norm_attn, bf16[2048,256]{1,0:T(8,128)(2,1)S(1)} %copy-done, bf16[2,2048,128]{2,1,0:T(8,128)(2,1)S(1)} %copy-done.1, bf16[256,2048]{1,0:T(8,128)(2,1)S(1)} %copy-done.2, ...), custom_call_target="tpu_custom_call" | custom-call | tf_op jit(solution)/shard_map/pallas_call | solution.py:272
  108.1 0.6 copy.16
Async XLA Ops:
  0.0 5.2 %copy-start.7 = (bf16[1024,32]{0,1:T(8,128)(2,1)S(1)}, bf16[1024,32]{0,1:T(8,128)(2,1)}, u32[]{:S(2)}) copy-start(bf16[1024,32]{0,1:T(8,128)(2,1)} %param.23) | copy-start | bytes 196612
  5.2 0.8 copy-start.4
  5.2 0.9 copy-start.5
  5.2 0.9 copy-start.6
  6.1 1.2 %copy-start = (bf16[2048,256]{1,0:T(8,128)(2,1)S(1)}, bf16[2048,256]{1,0:T(8,128)(2,1)}, u32[]{:S(2)}) copy-start(bf16[2048,256]{1,0:T(8,128)(2,1)} %wq.1) | copy-start | bytes 3145732
  7.3 1.2 %copy-start.1 = (bf16[2,2048,128]{2,1,0:T(8,128)(2,1)S(1)}, bf16[2,2048,128]{2,1,0:T(8,128)(2,1)}, u32[]{:S(2)}) copy-start(bf16[2,2048,128]{2,1,0:T(8,128)(2,1)} %wkv.1) | copy-start | bytes 3145732
  8.5 1.2 %copy-start.2 = (bf16[256,2048]{1,0:T(8,128)(2,1)S(1)}, bf16[256,2048]{1,0:T(8,128)(2,1)}, u32[]{:S(2)}) copy-start(bf16[256,2048]{1,0:T(8,128)(2,1)} %wo.1) | copy-start | bytes 3145732
  9.7 1.2 %copy-start.3 = (bf16[2,16,128,128]{3,2,1,0:T(8,128)(2,1)S(1)}, bf16[2,16,128,128]{3,2,1,0:T(8,128)(2,1)}, u32[]{:S(2)}) copy-start(bf16[2,16,128,128]{3,2,1,0:T(8,128)(2,1)} %param.17) | copy-start | bytes 3145732

commit v3 on v2

--- a/solution.py
+++ b/solution.py
@@ -27,14 +27,37 @@
     return (x * lax.rsqrt(mean_square + EPSILON) * gain).astype(BF16)
 
 
+def turned(angles):
+    turns = jnp.floor(angles * (2.0 / math.pi) + 0.5)
+    rest = ((angles - turns * 1.5703125) - turns * 4.837512969970703125e-4) - turns * 7.54978995489188216e-8
+    square = rest * rest
+    sine = rest + rest * square * (
+        -1.6666654611e-1 + square * (8.3321608736e-3 - 1.9515295891e-4 * square)
+    )
+    cosine = 1.0 - 0.5 * square + square * square * (
+        4.166664568298827e-2 + square * (-1.388731625493765e-3 + 2.443315711809948e-5 * square)
+    )
+    quadrant = turns - 4.0 * jnp.floor(turns * 0.25)
+    odd = (quadrant == 1.0) | (quadrant == 3.0)
+    cos_sign = jnp.where((quadrant == 1.0) | (quadrant == 2.0), -1.0, 1.0)
+    sin_sign = jnp.where(quadrant >= 2.0, -1.0, 1.0)
+    return jnp.where(odd, sine, cosine) * cos_sign, jnp.where(odd, cosine, sine) * sin_sign
+
+
+def flat(tile):
+    return jnp.concatenate([tile[i : i + 1] for i in range(tile.shape[0])], axis=1)
+
+
 def layer_kernel(
     pool, kv,
-    hidden, norm_attn, wq, wkv, wo, cache, owner, cosine, sine, norm_mlp, w_gate, w_up, w_down,
+    slot_entry, lengths, hidden_hbm, norm_attn_hbm, wq_hbm, wkv_hbm, wo_hbm, cache_hbm,
+    norm_mlp_hbm, w_gate, w_up, w_down,
     out,
+    hidden, norm_attn, norm_mlp, wq, wkv, wo, cache,
     wide, gate_pad, up_pad, down_pad,
     q_send, q_recv, part_send, part_recv, proj_send, proj_recv, in_send, in_recv,
     gu_send, gu_recv, act_send, act_recv, down_send, down_recv, fin_send, fin_recv,
-    send_sem, recv_sem,
+    send_sem, recv_sem, load_sem,
 ):
     me = lax.axis_index("pool")
     my_kv = lax.axis_index("kv")
@@ -54,12 +77,30 @@
         )
         return carry
 
-    lax.fori_loop(1, pool, greet_pool, 0)
-    lax.fori_loop(1, kv, greet_kv, 0)
-
-    def scatter(phase, source_of, target, axis, count, mine):
-        def body(k, carry):
-            peer = lax.rem(mine + k, count)
+    loads = [
+        pltpu.make_async_copy(source, target, load_sem.at[i])
+        for i, (source, target) in enumerate(
+            [(hidden_hbm, hidden), (norm_attn_hbm, norm_attn), (wq_hbm, wq), (wkv_hbm, wkv),
+             (cache_hbm, cache), (wo_hbm, wo), (norm_mlp_hbm, norm_mlp)]
+            + [
+                (source, target.at[pl.ds(32 * g, 32), :])
+                for source, target in ((w_gate, gate_pad), (w_up, up_pad), (w_down, down_pad))
+                for g in range(4)
+            ]
+        )
+    ]
+    for load in loads[:4]:
+        load.start()
+    lax.fori_loop(1, pool, greet_pool, 0, unroll=9)
+    lax.fori_loop(1, kv, greet_kv, 0, unroll=7)
+    for load in loads[4:]:
+        load.start()
+
+    my_y = me // 16
+    my_z = lax.rem(me, 16)
+
+    def scatter(phase, source_of, target, axis, mine):
+        def send(peer):
             pltpu.make_async_remote_copy(
                 src_ref=source_of(peer),
                 dst_ref=target.at[mine],
@@ -68,9 +109,25 @@
                 device_id={axis: peer},
                 device_id_type=MESH,
             ).start()
+
+        if axis == "kv":
+            for k in range(1, kv):
+                send(lax.rem(mine + k, kv))
+            return
+
+        def at(dy, z):
+            send(lax.rem(my_y + dy, 4) * 16 + z)
+
+        def body(t, carry):
+            step = (t + 1) // 2
+            z = lax.rem(my_z + 24 + (2 * lax.rem(t, 2) - 1) * step, 16)
+            for dy in (2, 1, 3, 0):
+                at(dy, z)
             return carry
 
-        lax.fori_loop(1, count, body, 0)
+        lax.fori_loop(0, 15, body, 0)
+        for dy in (2, 1, 3):
+            at(dy, my_z)
 
     def arrive(phase, target, count):
         view = target.at[pl.ds(0, count - 1)]
@@ -80,9 +137,25 @@
         view = target.at[pl.ds(0, count - 1)]
         pltpu.make_async_copy(view, view, send_sem.at[phase]).wait()
 
-    normed = rms(hidden[...].astype(F32), norm_attn[...].astype(F32))
-    cos_row = cosine[...]
-    sin_row = sine[...]
+    half_lane = lax.rem(lax.broadcasted_iota(jnp.int32, (1, LANES), 1), HEAD_SIZE // 2)
+    frequency = jnp.exp(half_lane.astype(F32) * (-2.0 * math.log(ROPE_BASE) / HEAD_SIZE))
+    position = jnp.full((1, LANES), lengths[me], jnp.int32).astype(F32)
+    cos_row, sin_row = turned(position * frequency)
+    lanes = lax.broadcasted_iota(jnp.int32, (1, LANES), 1)
+    sin_row = jnp.where(lanes < HEAD_SIZE // 2, -sin_row, sin_row)
+    owned = []
+    for i in range(slot_entry.shape[0]):
+        entry = slot_entry[i]
+        holder_of = jnp.maximum(entry, 0) // 64
+        left = lengths[holder_of] - (jnp.maximum(entry, 0) - holder_of * 64) * LANES
+        left = jnp.where(entry >= 0, left, 0)
+        owned.append(jnp.where(lanes < left, holder_of, -1))
+    owner = jnp.concatenate(owned, axis=1)
+    loads[0].wait()
+    loads[1].wait()
+    normed = rms(hidden[...].astype(F32), flat(norm_attn[...].astype(F32)))
+    loads[2].wait()
+    loads[3].wait()
 
     def rotated(v):
         return v * cos_row + pltpu.roll(v, HEAD_SIZE // 2, 1) * sin_row
@@ -98,27 +171,19 @@
     q_recv[me] = own_q
 
     pl.semaphore_wait(barrier, pool - 1 + kv - 1)
-    scatter(0, lambda peer: q_send.at[0], q_recv, "pool", pool, me)
-
-    for g in range(4):
-        here = quarter == g
-        gate_pad[pl.ds(32 * g, 32), :] = jnp.where(here, w_gate[...].astype(F32), 0.0).astype(BF16)
-        up_pad[pl.ds(32 * g, 32), :] = jnp.where(here, w_up[...].astype(F32), 0.0).astype(BF16)
-    place = (
-        lax.broadcasted_iota(jnp.int32, (32, LANES), 1)
-        == lax.broadcasted_iota(jnp.int32, (32, LANES), 0) + 32 * quarter
-    )
-    down_pad[...] = jnp.dot(
-        w_down[...], jnp.where(place, 1.0, 0.0).astype(BF16), preferred_element_type=F32
-    ).astype(BF16)
+    scatter(0, lambda peer: q_send.at[0], q_recv, "pool", me)
+
+    for load in loads[4:]:
+        load.wait()
+    own_lanes = lax.broadcasted_iota(jnp.int32, (pool, LANES), 1) // 32 == quarter
+    mlp_gain = flat(norm_mlp[...].astype(F32))
 
     arrive(0, q_recv, pool)
     every = q_recv[:, 0, :]
     rows = jnp.concatenate([every[:, :128], every[:, 128:]], axis=0).astype(BF16)
-    tokens = cache.shape[1]
     scores = lax.dot_general(rows, cache[0], (((1,), (1,)), ((), ())), preferred_element_type=F32)
     row_owner = lax.rem(lax.broadcasted_iota(jnp.int32, (2 * pool, 1), 0), pool)
-    taken = row_owner == owner[...]
+    taken = row_owner == owner
     scores = jnp.where(taken, scores, NEGATIVE)
     row_max = jnp.max(scores, axis=1, keepdims=True)
     raised = jnp.where(taken, jnp.exp(scores - row_max), 0.0)
@@ -145,7 +210,7 @@
 
     spread(part_send, 384)
     part_recv[me] = part_send[me]
-    scatter(1, lambda peer: part_send.at[peer], part_recv, "pool", pool, me)
+    scatter(1, lambda peer: part_send.at[peer], part_recv, "pool", me)
 
     arrive(1, part_recv, pool)
     parts = part_recv[:, 0, :]
@@ -164,21 +229,21 @@
     projected = jnp.dot(attended, wo[...], preferred_element_type=F32)
     proj_send[0] = projected
     proj_recv[my_kv] = projected
-    scatter(2, lambda peer: proj_send.at[0], proj_recv, "kv", kv, my_kv)
+    scatter(2, lambda peer: proj_send.at[0], proj_recv, "kv", my_kv)
     arrive(2, proj_recv, kv)
     total = proj_recv[0]
     for k in range(1, kv):
         total = total + proj_recv[k]
     residual = rounded(hidden[...].astype(F32) + total)
-    mlp_in = rms(residual, norm_mlp[...].astype(F32)).astype(F32)
+    mlp_in = rms(residual, mlp_gain).astype(F32)
     groups = mlp_in.shape[1] // LANES
     for g in range(groups):
         in_send[g] = mlp_in[:, g * LANES : (g + 1) * LANES]
     in_recv[me] = in_send[me // 4]
-    scatter(3, lambda peer: in_send.at[peer // 4], in_recv, "pool", pool, me)
+    scatter(3, lambda peer: in_send.at[peer // 4], in_recv, "pool", me)
 
     arrive(3, in_recv, pool)
-    columns = in_recv[:, 0, :].astype(BF16)
+    columns = jnp.where(own_lanes, in_recv[:, 0, :], 0.0).astype(BF16)
     half = w_gate.shape[1]
     wide[:, 0:half] = jnp.dot(columns, gate_pad[...], preferred_element_type=F32)
     wide[:, half : 2 * half] = jnp.dot(columns, up_pad[...], preferred_element_type=F32)
@@ -194,24 +259,29 @@
 
     lax.fori_loop(0, pool // 8, spread_gu, 0)
     gu_recv[me] = gu_send[me]
-    scatter(4, lambda peer: gu_send.at[peer], gu_recv, "pool", pool, me)
+    scatter(4, lambda peer: gu_send.at[peer], gu_recv, "pool", me)
     arrive(4, gu_recv, pool)
     summed = jnp.sum(gu_recv[...].astype(F32), axis=0)
     gate = summed[0:1]
     up = summed[1:2]
     activation = gate / (1.0 + jnp.exp(-gate)) * up
-    act_row = rounded(activation)
+    middle = half // 2
+    act_row = jnp.concatenate([activation[:, :middle], activation[:, middle:]], axis=0).astype(BF16)
     act_send[0] = act_row
     act_recv[me] = act_row
-    scatter(5, lambda peer: act_send.at[0], act_recv, "pool", pool, me)
+    scatter(5, lambda peer: act_send.at[0], act_recv, "pool", me)
 
     arrive(5, act_recv, pool)
-    activations = act_recv[:, 0, :].astype(BF16)
-    wide[:, 0:LANES] = jnp.dot(activations, down_pad[...], preferred_element_type=F32)
+    activations = act_recv[...].astype(F32)
+    activations = jnp.concatenate([activations[:, 0, :], activations[:, 1, :]], axis=1).astype(BF16)
+    down = lax.dot_general(
+        activations, down_pad[...], (((1,), (1,)), ((), ())), preferred_element_type=F32
+    )
+    wide[:, 0:LANES] = jnp.where(own_lanes, down, 0.0)
 
     spread(down_send, LANES)
     down_recv[me] = down_send[me]
-    scatter(6, lambda peer: down_send.at[peer], down_recv, "pool", pool, me)
+    scatter(6, lambda peer: down_send.at[peer], down_recv, "pool", me)
     arrive(6, down_recv, pool)
     pieces = []
     for g in range(groups):
@@ -222,7 +292,7 @@
     down_row = jnp.concatenate(pieces, axis=1)
     fin_send[0] = down_row
     fin_recv[my_kv] = down_row
-    scatter(7, lambda peer: fin_send.at[0], fin_recv, "kv", kv, my_kv)
+    scatter(7, lambda peer: fin_send.at[0], fin_recv, "kv", my_kv)
     arrive(7, fin_recv, kv)
     total = fin_recv[0]
     for k in range(1, kv):
@@ -245,40 +315,27 @@
 ):
     width = hidden.shape[1]
     half = w_gate.shape[1]
-    home = lax.axis_index("pool")
-    slot_count = slot_entry.shape[0]
-    block_len = cache.shape[2]
-    requests = lengths.shape[0]
-    max_blocks = 64
-    position = lax.dynamic_slice_in_dim(lengths, home, 1).astype(F32)
-    halfway = HEAD_SIZE // 2
-    frequency = jnp.exp(
-        jnp.arange(halfway, dtype=F32) * (-2.0 * math.log(ROPE_BASE) / HEAD_SIZE)
-    )
-    angles = position[:, None] * frequency[None, :]
-    cosine = jnp.cos(angles)
-    sine = jnp.sin(angles)
-    cosine = jnp.concatenate([cosine, cosine], axis=1)
-    sine = jnp.concatenate([-sine, sine], axis=1)
-    live = slot_entry >= 0
-    owners = jnp.where(live, slot_entry // max_blocks, -1)
-    blocks = jnp.where(live, slot_entry % max_blocks, 0)
-    hit = owners[:, None] == jnp.arange(requests, dtype=jnp.int32)[None, :]
-    extent = jnp.sum(jnp.where(hit, lengths[None, :], 0), axis=1)
-    places = blocks[:, None] * block_len + jnp.arange(block_len, dtype=jnp.int32)[None, :]
-    owner = jnp.where(places < extent[:, None], owners[:, None], -1)
-    owner = owner.reshape(1, slot_count * block_len)
+    tokens = cache.shape[1] * cache.shape[2]
+    smem = pl.BlockSpec(memory_space=pltpu.SMEM)
+    hbm = pl.BlockSpec(memory_space=pltpu.HBM)
     vmem = pl.BlockSpec(memory_space=pltpu.VMEM)
     return pl.pallas_call(
         functools.partial(layer_kernel, pool, kv),
         out_shape=jax.ShapeDtypeStruct((1, width), BF16),
-        in_specs=[vmem] * 13,
+        in_specs=[smem] * 2 + [hbm] * 10,
         out_specs=vmem,
         scratch_shapes=[
+            pltpu.VMEM((1, width), BF16),
+            pltpu.VMEM((width // LANES, LANES), BF16),
+            pltpu.VMEM((width // LANES, LANES), BF16),
+            pltpu.VMEM(wq.shape, BF16),
+            pltpu.VMEM(wkv.shape, BF16),
+            pltpu.VMEM(wo.shape, BF16),
+            pltpu.VMEM((2, tokens, HEAD_SIZE), BF16),
             pltpu.VMEM((pool, 2 * half), F32),
             pltpu.VMEM((LANES, half), BF16),
             pltpu.VMEM((LANES, half), BF16),
-            pltpu.VMEM((half, LANES), BF16),
+            pltpu.VMEM((LANES, half), BF16),
             pltpu.VMEM((1, 1, 256), F32),
             pltpu.VMEM((pool, 1, 256), F32),
             pltpu.VMEM((pool, 1, 384), F32),
@@ -289,22 +346,23 @@
             pltpu.VMEM((pool, 1, LANES), F32),
             pltpu.VMEM((pool, 2, half), BF16),
             pltpu.VMEM((pool, 2, half), BF16),
-            pltpu.VMEM((1, 1, half), F32),
-            pltpu.VMEM((pool, 1, half), F32),
+            pltpu.VMEM((1, 2, half // 2), BF16),
+            pltpu.VMEM((pool, 2, half // 2), BF16),
             pltpu.VMEM((pool, 1, LANES), F32),
             pltpu.VMEM((pool, 1, LANES), F32),
             pltpu.VMEM((1, 1, width), F32),
             pltpu.VMEM((kv, 1, width), F32),
             pltpu.SemaphoreType.DMA((8,)),
             pltpu.SemaphoreType.DMA((8,)),
+            pltpu.SemaphoreType.DMA((19,)),
         ],
         compiler_params=pltpu.CompilerParams(
-            collective_id=0, has_side_effects=True, vmem_limit_bytes=48 * 1024 * 1024
+            collective_id=0, has_side_effects=True, vmem_limit_bytes=67043328
         ),
     )(
-        hidden, norm_attn.reshape(1, width), wq, wkv, wo,
-        cache.reshape(2, slot_count * block_len, HEAD_SIZE), owner, cosine, sine,
-        norm_mlp.reshape(1, width), w_gate, w_up, w_down,
+        slot_entry, lengths, hidden, norm_attn.reshape(width // LANES, LANES), wq, wkv, wo,
+        cache.reshape(2, tokens, HEAD_SIZE), norm_mlp.reshape(width // LANES, LANES),
+        w_gate, w_up, w_down.T,
     )
 
 

time: 109 us -> 87.1 us (0.80)
  Pallas kernels: 97.1 us -> 85.6 us
  local copies, waits for them, and re-layouts: 9.01 us -> 1.3 us
  other arithmetic: 1.84 us -> 0 us
    pallas_call x1, Pallas kernels: 97.1 us -> 85.6 us  [per_device(): pl.pallas_call(functools.partial(layer_kernel, pool, kv), out_shape=jax.S...]
    unnamed x18 -> x1, local copies, waits for them, and re-layouts: 6.35 us -> 1.3 us
    reshape x2 -> x0, local copies, waits for them, and re-layouts: 1.39 us -> none  [the longest x1 0.7 us: per_device(): norm_attn.reshape(1, width)]
    dynamic_slice x1 -> x0, local copies, waits for them, and re-layouts: 1.27 us -> none  [per_device(): position = lax.dynamic_slice_in_dim(lengths, home, 1).astype(F32)]
where the time goes in v3:
time: 87.1 us; the launch traced here: 87 us
  Pallas kernels  85.6 us (98%)
  local copies, waits for them, and re-layouts  1.3 us (1%)
    pallas_call x1, Pallas kernels, per_device(): pl.pallas_call(functools.partial(layer_kernel, pool, kv), out_shape=jax.S...  85.6 us

profile of v3, /device:TPU:1, one launch (start us, length us, event | category | flops | bytes accessed | tf_op | source)
XLA Modules:
  0.0 87.0 jit_solution(8193602465093096220)
XLA Ops:
  0.0 85.6 %shard_map.118 = bf16[1,2048]{1,0:T(2,128)(2,1)} custom-call(s32[16]{0:T(128)} %slot_entry.1, s32[64]{0:T(128)} %lengths.1, bf16[1,2048]{1,0:T(2,128)(2,1)} %hidden_hbm.1, bf16[16,128]{1,0:T(8,128)(2,1)} %bitcast.6, bf16[2048,256]{1,0:T(8,128)(2,1)} %wq_hbm.1, bf16[2,2048,128]{2,1,0:T(8,128)(2,1)} %wkv_hbm.1, bf16[256,2048]{1,0:T(8,128)(2,1)} %wo_hbm.1, ...), custom_call_target="tpu_custom_call" | custom-call | tf_op jit(solution)/shard_map/pallas_call | solution.py:322
  85.7 1.3 %copy.14 = bf16[1,2048]{1,0:T(2,128)(2,1)} copy(bf16[1,2048]{1,0:T(2,128)(2,1)} %shard_map.118) | data formatting | bytes 8192

commit v4 on v3

--- a/solution.py
+++ b/solution.py
@@ -56,7 +56,7 @@
     hidden, norm_attn, norm_mlp, wq, wkv, wo, cache,
     wide, gate_pad, up_pad, down_pad,
     q_send, q_recv, part_send, part_recv, proj_send, proj_recv, in_send, in_recv,
-    gu_send, gu_recv, act_send, act_recv, down_send, down_recv, fin_send, fin_recv,
+    gu_send, gu_mid, gu_half, gu_recv, act_send, act_recv, down_send, down_recv, fin_send, fin_recv,
     send_sem, recv_sem, load_sem,
 ):
     me = lax.axis_index("pool")
@@ -248,19 +248,43 @@
     wide[:, 0:half] = jnp.dot(columns, gate_pad[...], preferred_element_type=F32)
     wide[:, half : 2 * half] = jnp.dot(columns, up_pad[...], preferred_element_type=F32)
 
-    def spread_gu(b, carry):
+    def spread_gu(b):
         at = pl.ds(pl.multiple_of(b * 8, 8), 8)
         gate_rows = wide[at, 0:half]
         up_rows = wide[at, half : 2 * half]
         for i in range(8):
             both = jnp.concatenate([gate_rows[i : i + 1], up_rows[i : i + 1]], axis=0)
             gu_send[b * 8 + i] = both.astype(BF16)
-        return carry
-
-    lax.fori_loop(0, pool // 8, spread_gu, 0)
-    gu_recv[me] = gu_send[me]
-    scatter(4, lambda peer: gu_send.at[peer], gu_recv, "pool", me)
-    arrive(4, gu_recv, pool)
+
+    def send_to(source, target, phase, peer):
+        pltpu.make_async_remote_copy(
+            src_ref=source,
+            dst_ref=target,
+            send_sem=send_sem.at[phase],
+            recv_sem=recv_sem.at[phase],
+            device_id={"pool": peer},
+            device_id_type=MESH,
+        ).start()
+
+    def along_z(source_of, target, phase):
+        for dz in (8, 9, 7, 10, 6, 11, 5, 12, 4, 13, 3, 14, 2, 15, 1):
+            z = lax.rem(my_z + dz, 16)
+            send_to(source_of(z), target, phase, my_y * 16 + z)
+
+    for dy in (2, 1, 3, 0):
+        there = lax.rem(my_y + dy, 4)
+        spread_gu(2 * there)
+        spread_gu(2 * there + 1)
+        if dy:
+            send_to(
+                gu_send.at[pl.ds(16 * there, 16)], gu_mid.at[my_y], 4, 16 * there + my_z
+            )
+    gu_mid[my_y] = gu_send[pl.ds(16 * my_y, 16)]
+    arrive(4, gu_mid, 4)
+    gu_half[...] = jnp.sum(gu_mid[...].astype(F32), axis=0).astype(BF16)
+    along_z(lambda z: gu_half.at[z], gu_recv.at[my_z], 8)
+    gu_recv[my_z] = gu_half[my_z]
+    arrive(8, gu_recv, 16)
     summed = jnp.sum(gu_recv[...].astype(F32), axis=0)
     gate = summed[0:1]
     up = summed[1:2]
@@ -268,11 +292,15 @@
     middle = half // 2
     act_row = jnp.concatenate([activation[:, :middle], activation[:, middle:]], axis=0).astype(BF16)
     act_send[0] = act_row
-    act_recv[me] = act_row
-    scatter(5, lambda peer: act_send.at[0], act_recv, "pool", me)
-
-    arrive(5, act_recv, pool)
-    activations = act_recv[...].astype(F32)
+    along_z(lambda z: act_send.at[0], act_recv.at[my_y, my_z], 5)
+    act_recv[my_y, my_z] = act_row
+    arrive(5, act_recv.at[0], 16)
+    for dy in (2, 1, 3):
+        there = lax.rem(my_y + dy, 4)
+        send_to(act_recv.at[my_y], act_recv.at[my_y], 9, 16 * there + my_z)
+
+    arrive(9, act_recv, 4)
+    activations = act_recv[...].astype(F32).reshape(pool, 2, middle)
     activations = jnp.concatenate([activations[:, 0, :], activations[:, 1, :]], axis=1).astype(BF16)
     down = lax.dot_general(
         activations, down_pad[...], (((1,), (1,)), ((), ())), preferred_element_type=F32
@@ -303,8 +331,10 @@
     sent(1, part_recv, pool)
     sent(2, proj_recv, kv)
     sent(3, in_recv, pool)
-    sent(4, gu_recv, pool)
-    sent(5, act_recv, pool)
+    sent(4, gu_mid, 4)
+    sent(8, gu_recv, 16)
+    sent(5, act_recv.at[0], 16)
+    sent(9, act_recv, 4)
     sent(6, down_recv, pool)
     sent(7, fin_recv, kv)
 
@@ -345,15 +375,17 @@
             pltpu.VMEM((width // LANES, 1, LANES), F32),
             pltpu.VMEM((pool, 1, LANES), F32),
             pltpu.VMEM((pool, 2, half), BF16),
-            pltpu.VMEM((pool, 2, half), BF16),
+            pltpu.VMEM((4, 16, 2, half), BF16),
+            pltpu.VMEM((16, 2, half), BF16),
+            pltpu.VMEM((16, 2, half), BF16),
             pltpu.VMEM((1, 2, half // 2), BF16),
-            pltpu.VMEM((pool, 2, half // 2), BF16),
+            pltpu.VMEM((4, 16, 2, half // 2), BF16),
             pltpu.VMEM((pool, 1, LANES), F32),
             pltpu.VMEM((pool, 1, LANES), F32),
             pltpu.VMEM((1, 1, width), F32),
             pltpu.VMEM((kv, 1, width), F32),
-            pltpu.SemaphoreType.DMA((8,)),
-            pltpu.SemaphoreType.DMA((8,)),
+            pltpu.SemaphoreType.DMA((10,)),
+            pltpu.SemaphoreType.DMA((10,)),
             pltpu.SemaphoreType.DMA((19,)),
         ],
         compiler_params=pltpu.CompilerParams(

time: 87.1 us -> 87 us (level)
  no operation moved by 1% of the time
where the time goes in v4:
time: 87 us; the launch traced here: 86.8 us
  Pallas kernels  85.5 us (98%)
  local copies, waits for them, and re-layouts  1.3 us (1%)
    pallas_call x1, Pallas kernels, per_device(): pl.pallas_call(functools.partial(layer_kernel, pool, kv), out_shape=jax.S...  85.5 us

profile of v4, /device:TPU:1, one launch (start us, length us, event | category | flops | bytes accessed | tf_op | source)
XLA Modules:
  0.0 86.8 jit_solution(13497133508958156627)
XLA Ops:
  0.0 85.5 %shard_map.118 = bf16[1,2048]{1,0:T(2,128)(2,1)} custom-call(s32[16]{0:T(128)} %slot_entry.1, s32[64]{0:T(128)} %lengths.1, bf16[1,2048]{1,0:T(2,128)(2,1)} %hidden_hbm.1, bf16[16,128]{1,0:T(8,128)(2,1)} %bitcast.6, bf16[2048,256]{1,0:T(8,128)(2,1)} %wq_hbm.1, bf16[2,2048,128]{2,1,0:T(8,128)(2,1)} %wkv_hbm.1, bf16[256,2048]{1,0:T(8,128)(2,1)} %wo_hbm.1, ...), custom_call_target="tpu_custom_call" | custom-call | tf_op jit(solution)/shard_map/pallas_call | solution.py:352
  85.5 1.3 %copy.14 = bf16[1,2048]{1,0:T(2,128)(2,1)} copy(bf16[1,2048]{1,0:T(2,128)(2,1)} %shard_map.118) | data formatting | bytes 8192

commit v5 on v4

--- a/solution.py
+++ b/solution.py
@@ -125,7 +125,7 @@
                 at(dy, z)
             return carry
 
-        lax.fori_loop(0, 15, body, 0)
+        lax.fori_loop(0, 15, body, 0, unroll=3)
         for dy in (2, 1, 3):
             at(dy, my_z)
 
@@ -166,7 +166,7 @@
     q1 = rounded(rotated(q[:, 128:]) * scale)
     new_key = rounded(rotated(jnp.dot(normed, wkv[0], preferred_element_type=F32)))
     new_value = rounded(jnp.dot(normed, wkv[1], preferred_element_type=F32))
-    own_q = jnp.concatenate([q0, q1], axis=1)
+    own_q = jnp.concatenate([q0, q1], axis=0).astype(BF16)
     q_send[0] = own_q
     q_recv[me] = own_q
 
@@ -179,8 +179,8 @@
     mlp_gain = flat(norm_mlp[...].astype(F32))
 
     arrive(0, q_recv, pool)
-    every = q_recv[:, 0, :]
-    rows = jnp.concatenate([every[:, :128], every[:, 128:]], axis=0).astype(BF16)
+    every = q_recv[...].astype(F32)
+    rows = jnp.concatenate([every[:, 0, :], every[:, 1, :]], axis=0).astype(BF16)
     scores = lax.dot_general(rows, cache[0], (((1,), (1,)), ((), ())), preferred_element_type=F32)
     row_owner = lax.rem(lax.broadcasted_iota(jnp.int32, (2 * pool, 1), 0), pool)
     taken = row_owner == owner
@@ -292,15 +292,11 @@
     middle = half // 2
     act_row = jnp.concatenate([activation[:, :middle], activation[:, middle:]], axis=0).astype(BF16)
     act_send[0] = act_row
-    along_z(lambda z: act_send.at[0], act_recv.at[my_y, my_z], 5)
-    act_recv[my_y, my_z] = act_row
-    arrive(5, act_recv.at[0], 16)
-    for dy in (2, 1, 3):
-        there = lax.rem(my_y + dy, 4)
-        send_to(act_recv.at[my_y], act_recv.at[my_y], 9, 16 * there + my_z)
-
-    arrive(9, act_recv, 4)
-    activations = act_recv[...].astype(F32).reshape(pool, 2, middle)
+    act_recv[me] = act_row
+    scatter(5, lambda peer: act_send.at[0], act_recv, "pool", me)
+
+    arrive(5, act_recv, pool)
+    activations = act_recv[...].astype(F32)
     activations = jnp.concatenate([activations[:, 0, :], activations[:, 1, :]], axis=1).astype(BF16)
     down = lax.dot_general(
         activations, down_pad[...], (((1,), (1,)), ((), ())), preferred_element_type=F32
@@ -333,8 +329,7 @@
     sent(3, in_recv, pool)
     sent(4, gu_mid, 4)
     sent(8, gu_recv, 16)
-    sent(5, act_recv.at[0], 16)
-    sent(9, act_recv, 4)
+    sent(5, act_recv, pool)
     sent(6, down_recv, pool)
     sent(7, fin_recv, kv)
 
@@ -366,8 +361,8 @@
             pltpu.VMEM((LANES, half), BF16),
             pltpu.VMEM((LANES, half), BF16),
             pltpu.VMEM((LANES, half), BF16),
-            pltpu.VMEM((1, 1, 256), F32),
-            pltpu.VMEM((pool, 1, 256), F32),
+            pltpu.VMEM((1, 2, HEAD_SIZE), BF16),
+            pltpu.VMEM((pool, 2, HEAD_SIZE), BF16),
             pltpu.VMEM((pool, 1, 384), F32),
             pltpu.VMEM((pool, 1, 384), F32),
             pltpu.VMEM((1, 1, width), F32),
@@ -379,13 +374,13 @@
             pltpu.VMEM((16, 2, half), BF16),
             pltpu.VMEM((16, 2, half), BF16),
             pltpu.VMEM((1, 2, half // 2), BF16),
-            pltpu.VMEM((4, 16, 2, half // 2), BF16),
+            pltpu.VMEM((pool, 2, half // 2), BF16),
             pltpu.VMEM((pool, 1, LANES), F32),
             pltpu.VMEM((pool, 1, LANES), F32),
             pltpu.VMEM((1, 1, width), F32),
             pltpu.VMEM((kv, 1, width), F32),
-            pltpu.SemaphoreType.DMA((10,)),
-            pltpu.SemaphoreType.DMA((10,)),
+            pltpu.SemaphoreType.DMA((9,)),
+            pltpu.SemaphoreType.DMA((9,)),
             pltpu.SemaphoreType.DMA((19,)),
         ],
         compiler_params=pltpu.CompilerParams(

time: 87 us -> 84.4 us (0.970)
  Pallas kernels: 85.5 us -> 82.9 us
    pallas_call x1, Pallas kernels: 85.5 us -> 82.9 us  [per_device(): pl.pallas_call(functools.partial(layer_kernel, pool, kv), out_shape=jax.S...]
where the time goes in v5:
time: 84.4 us; the launch traced here: 84.2 us
  Pallas kernels  82.9 us (98%)
  local copies, waits for them, and re-layouts  1.3 us (2%)
    pallas_call x1, Pallas kernels, per_device(): pl.pallas_call(functools.partial(layer_kernel, pool, kv), out_shape=jax.S...  82.9 us

profile of v5, /device:TPU:1, one launch (start us, length us, event | category | flops | bytes accessed | tf_op | source)
XLA Modules:
  0.0 84.2 jit_solution(674955723890404891)
XLA Ops:
  0.0 82.9 %shard_map.118 = bf16[1,2048]{1,0:T(2,128)(2,1)} custom-call(s32[16]{0:T(128)} %slot_entry.1, s32[64]{0:T(128)} %lengths.1, bf16[1,2048]{1,0:T(2,128)(2,1)} %hidden_hbm.1, bf16[16,128]{1,0:T(8,128)(2,1)} %bitcast.6, bf16[2048,256]{1,0:T(8,128)(2,1)} %wq_hbm.1, bf16[2,2048,128]{2,1,0:T(8,128)(2,1)} %wkv_hbm.1, bf16[256,2048]{1,0:T(8,128)(2,1)} %wo_hbm.1, ...), custom_call_target="tpu_custom_call" | custom-call | tf_op jit(solution)/shard_map/pallas_call | solution.py:347
  82.9 1.3 %copy.14 = bf16[1,2048]{1,0:T(2,128)(2,1)} copy(bf16[1,2048]{1,0:T(2,128)(2,1)} %shard_map.118) | data formatting | bytes 8192

commit v6 on v5

--- a/solution.py
+++ b/solution.py
@@ -65,17 +65,30 @@
 
     barrier = pltpu.get_barrier_semaphore()
 
-    def greet_pool(k, carry):
+    my_y = me // 16
+    my_z = lax.rem(me, 16)
+
+    def far_z(t):
+        return lax.rem(my_z + 24 + (2 * lax.rem(t, 2) - 1) * ((t + 1) // 2), 16)
+
+    def greet(dy, z):
         pl.semaphore_signal(
-            barrier, inc=1, device_id={"pool": lax.rem(me + k, pool)}, device_id_type=MESH
+            barrier, inc=1, device_id={"pool": lax.rem(my_y + dy, 4) * 16 + z}, device_id_type=MESH
         )
+
+    def greet_far(t, carry):
+        z = far_z(t)
+        for dy in (2, 1, 3, 0):
+            greet(dy, z)
         return carry
 
-    def greet_kv(k, carry):
+    lax.fori_loop(0, 15, greet_far, 0, unroll=3)
+    for dy in (2, 1, 3):
+        greet(dy, my_z)
+    for k in range(1, kv):
         pl.semaphore_signal(
             barrier, inc=1, device_id={"kv": lax.rem(my_kv + k, kv)}, device_id_type=MESH
         )
-        return carry
 
     loads = [
         pltpu.make_async_copy(source, target, load_sem.at[i])
@@ -89,15 +102,8 @@
             ]
         )
     ]
-    for load in loads[:4]:
+    for load in loads:
         load.start()
-    lax.fori_loop(1, pool, greet_pool, 0, unroll=9)
-    lax.fori_loop(1, kv, greet_kv, 0, unroll=7)
-    for load in loads[4:]:
-        load.start()
-
-    my_y = me // 16
-    my_z = lax.rem(me, 16)
 
     def scatter(phase, source_of, target, axis, mine):
         def send(peer):
@@ -119,8 +125,7 @@
             send(lax.rem(my_y + dy, 4) * 16 + z)
 
         def body(t, carry):
-            step = (t + 1) // 2
-            z = lax.rem(my_z + 24 + (2 * lax.rem(t, 2) - 1) * step, 16)
+            z = far_z(t)
             for dy in (2, 1, 3, 0):
                 at(dy, z)
             return carry

time: 84.4 us -> 84.3 us (level)
  no operation moved by 1% of the time
where the time goes in v6:
time: 84.3 us; the launch traced here: 84 us
  Pallas kernels  82.7 us (98%)
  local copies, waits for them, and re-layouts  1.3 us (2%)
    pallas_call x1, Pallas kernels, per_device(): pl.pallas_call(functools.partial(layer_kernel, pool, kv), out_shape=jax.S...  82.7 us

profile of v6, /device:TPU:1, one launch (start us, length us, event | category | flops | bytes accessed | tf_op | source)
XLA Modules:
  0.0 84.0 jit_solution(10173958962776364702)
XLA Ops:
  0.0 82.7 %shard_map.118 = bf16[1,2048]{1,0:T(2,128)(2,1)} custom-call(s32[16]{0:T(128)} %slot_entry.1, s32[64]{0:T(128)} %lengths.1, bf16[1,2048]{1,0:T(2,128)(2,1)} %hidden_hbm.1, bf16[16,128]{1,0:T(8,128)(2,1)} %bitcast.6, bf16[2048,256]{1,0:T(8,128)(2,1)} %wq_hbm.1, bf16[2,2048,128]{2,1,0:T(8,128)(2,1)} %wkv_hbm.1, bf16[256,2048]{1,0:T(8,128)(2,1)} %wo_hbm.1, ...), custom_call_target="tpu_custom_call" | custom-call | tf_op jit(solution)/shard_map/pallas_call | solution.py:352
  82.7 1.3 %copy.14 = bf16[1,2048]{1,0:T(2,128)(2,1)} copy(bf16[1,2048]{1,0:T(2,128)(2,1)} %shard_map.118) | data formatting | bytes 8192
